TPU v7x, 512 devices: a whole 4x8x8 slice. The times are simulated.
512 devices in a mesh: row: 8 (over z), col: 16 (over y, core), vox: 4 (over x).
Axes of the slice: x: 4, y: 8, z: 8, core: 2. Of those that a mesh axis runs over, the one named last changes fastest.
Arguments:
- panel_top: bfloat16 [1024, 1024], P('row', ('col', 'vox')), may hold values from -0.059814453 to 0.059814453
- panel_low: bfloat16 [8192, 1024], P('row', ('col', 'vox')), may hold values from -1.1953125 to 1.1953125
- panel_next: bfloat16 [8192, 1024], P('row', ('col', 'vox')), may hold values from -1.1953125 to 1.1953125
- gram_rest: bfloat16 [8192, 8192], P('row', ('col', 'vox')), may hold values from -18 to 18
- inverses: bfloat16 [2, 1024, 1024], P(None, 'row'), as said below
- right_top: bfloat16 [2, 1024, 8192], P(None, None, ('col', 'vox')), may hold values from -1.796875 to 1.796875
- right_low: bfloat16 [8192, 8192], P('row', ('col', 'vox')), may hold values from -24 to 24
Outputs:
- factor: bfloat16 [2, 8192, 1024], P(None, 'row', ('col', 'vox'))
- solved: bfloat16 [2, 1024, 8192], P(None, None, ('col', 'vox'))
- trailing: float32 [8192, 8192], P('row', ('col', 'vox'))
- residual: float32 [8192, 8192], P('row', ('col', 'vox'))
Inputs may be any that keep to these rules, and one draw needn't show every extreme that they name: Each inverses[k] is lower triangular with diagonal entries from 1 to 2.
All inputs are finite; a program needn't handle non-finite values.
Results may differ from a plain program's by a relative error of at most 0.0057.
Values may be sent and summed in bfloat16 or wider, within the bound.
No kernel may reach another device: no remote copies, remote signals or barrier semaphores. Data moves between devices by JAX's collectives and lax.ppermute only.
A program may use at most 64 MiB of HBM per device.

v0:
```python
import jax
import jax.numpy as jnp
from jax import lax
from jax.sharding import PartitionSpec as P


def spread(block, axis, source):
    block = jnp.where(lax.axis_index(axis) == source, block, jnp.zeros_like(block))
    return lax.psum(block, axis)


def contract(left, right):
    return lax.dot_general(
        left, right, (((1,), (1,)), ((), ())), preferred_element_type=jnp.float32
    )


def per_device(panel_top, panel_low, panel_next, gram_rest, inverses, right_top, right_low):
    col_index = lax.axis_index(("col", "vox"))
    row_index = lax.axis_index("row")
    col_width = panel_low.shape[1]
    top_rows = panel_top.shape[0]
    low_rows = panel_low.shape[0]
    rest_cols = gram_rest.shape[1]
    root_row = col_index * rest_cols // low_rows
    whole_inverses = lax.all_gather(inverses, "row", axis=1, tiled=True)
    own_rows = lax.dynamic_slice_in_dim(whole_inverses, col_index * col_width, col_width, 1)
    rows_used = own_rows[0]
    own_top = contract(lax.all_gather(panel_top, ("col", "vox"), axis=1, tiled=True), rows_used)
    own_low = contract(lax.all_gather(panel_low, ("col", "vox"), axis=1, tiled=True), rows_used)
    first_top, first_low = (
        lax.all_gather(own_top.astype(jnp.bfloat16), ("col", "vox"), axis=1, tiled=True),
        lax.all_gather(own_low.astype(jnp.bfloat16), ("col", "vox"), axis=1, tiled=True),
    )
    outgoing = (
        lax.dynamic_slice_in_dim(
            first_top, col_index * col_width - root_row * top_rows, col_width, 0
        ),
        lax.dynamic_slice_in_dim(
            first_low, col_index * rest_cols - root_row * low_rows, rest_cols, 0
        ),
    )
    owner_top, owner_low = (
        spread(outgoing[0], "row", root_row),
        spread(outgoing[1], "row", root_row),
    )
    updated = (panel_next.astype(jnp.float32) - contract(first_low, owner_top)).astype(jnp.bfloat16)
    rows_used = own_rows[1]
    own_next = contract(lax.all_gather(updated, ("col", "vox"), axis=1, tiled=True), rows_used)
    second_low = lax.all_gather(own_next.astype(jnp.bfloat16), ("col", "vox"), axis=1, tiled=True)
    owner_next = spread(
        lax.dynamic_slice_in_dim(
            second_low, col_index * rest_cols - root_row * low_rows, rest_cols, 0
        ),
        "row",
        root_row,
    )
    trailing = (
        gram_rest.astype(jnp.float32)
        - contract(first_low, owner_low)
        - contract(second_low, owner_next)
    )
    first_solve = jnp.dot(
        whole_inverses[0], right_top[0], preferred_element_type=jnp.float32
    ).astype(jnp.bfloat16)
    top_slice = lax.dynamic_slice_in_dim(right_top[1], row_index * top_rows, top_rows, 0)
    top_part = (
        top_slice.astype(jnp.float32)
        - jnp.dot(first_top, first_solve, preferred_element_type=jnp.float32)
    ).astype(jnp.bfloat16)
    top_new = lax.all_gather(top_part, "row", axis=0, tiled=True)
    second_solve = jnp.dot(whole_inverses[1], top_new, preferred_element_type=jnp.float32).astype(
        jnp.bfloat16
    )
    residual = (
        right_low.astype(jnp.float32)
        - jnp.dot(first_low, first_solve, preferred_element_type=jnp.float32)
        - jnp.dot(second_low, second_solve, preferred_element_type=jnp.float32)
    )
    factor = jnp.stack(
        [
            lax.dynamic_slice_in_dim(first_low, col_index * col_width, col_width, 1),
            lax.dynamic_slice_in_dim(second_low, col_index * col_width, col_width, 1),
        ]
    )
    solved = jnp.stack([first_solve, second_solve])
    return (factor, solved, trailing, residual)


def solution(mesh):
    in_specs = (
        P("row", ("col", "vox")),
        P("row", ("col", "vox")),
        P("row", ("col", "vox")),
        P("row", ("col", "vox")),
        P(None, "row", None),
        P(None, None, ("col", "vox")),
        P("row", ("col", "vox")),
    )
    out_specs = (
        P(None, "row", ("col", "vox")),
        P(None, None, ("col", "vox")),
        P("row", ("col", "vox")),
        P("row", ("col", "vox")),
    )
    return jax.shard_map(
        per_device, mesh=mesh, in_specs=in_specs, out_specs=out_specs, check_vma=False
    )
```

profile of v0, /device:TPU:2, one launch (start us, length us, event | category | flops | bytes accessed | tf_op | source)
XLA Modules:
  0.0 587.9 jit_solution(6978349543570293704)
XLA Ops:
  7.2 0.0 copy-start.7
  7.2 0.0 all-gather.8.cloned.1.call-start
  7.2 0.7 all-gather.8.cloned.1.call-update
  7.9 0.0 all-gather.6.cloned.1.call-start
  8.0 0.7 all-gather.6.cloned.1.call-update
  8.7 0.0 copy-start.6
  8.7 0.0 all-gather.10.cloned.1.call-start
  8.7 88.6 %all-gather.8.cloned.1.call-done = bf16[1024,1024]{0,1:T(8,128)(2,1)} async-done(((bf16[1024,16]{0,1:T(8,128)(2,1)}), bf16[1024,1024]{0,1:T(8,128)(2,1)}) %all-gather.8.cloned.1.call-update) | async-done | bytes 2097168 | tf_op jit(solution)/shard_map/all_gather | solution.py:30
  97.4 59.5 %all-gather.6.cloned.1.call-done = bf16[2,1024,1024]{2,1,0:T(8,128)(2,1)} async-done(((bf16[2,128,1024]{2,1,0:T(8,128)(2,1)}), bf16[2,1024,1024]{2,1,0:T(8,128)(2,1)}) %all-gather.6.cloned.1.call-update) | async-done | bytes 4194320 | tf_op jit(solution)/shard_map/all_gather | solution.py:26
  156.9 2.6 fusion.6
  159.5 0.0 all-gather.10.cloned.1.call-update
  159.5 0.0 all-gather.12.cloned.1.call-start
  159.6 0.0 copy-done.7
  159.6 69.7 %all_gather.27 = bf16[128,1024]{0,1:T(8,128)(2,1)S(1)} all-gather(bf16[128,16]{0,1:T(8,128)(2,1)S(1)} %copy-done.7), channel_id=1, replica_groups=mesh['row'=8,'col'=16,'vox'=4] {'col','vox'}, dimensions={1}, use_global_device_ids=true | all-gather | bytes 266240 | tf_op jit(solution)/shard_map/all_gather | solution.py:29
  229.3 0.9 fusion.7
  230.2 66.4 %all_gather.28 = bf16[128,1024]{0,1:T(8,128)(2,1)S(1)} all-gather(bf16[128,16]{0,1:T(8,128)(2,1)S(1)} %fusion.7), channel_id=1, replica_groups=mesh['row'=8,'col'=16,'vox'=4] {'col','vox'}, dimensions={1}, use_global_device_ids=true | all-gather | bytes 266240 | tf_op jit(solution)/shard_map/all_gather | solution.py:32
  296.6 0.1 dynamic-slice_select_fusion.2
  296.8 31.6 %psum.21 = bf16[16,1024]{0,1:T(8,128)(2,1)S(1)} all-reduce(bf16[16,1024]{0,1:T(8,128)(2,1)S(1)} %dynamic-slice_select_fusion.2), channel_id=1, replica_groups=mesh['row'=8,'col'=16,'vox'=4] {'row'}, use_global_device_ids=true, to_apply=%region_0.1 | all-reduce | flops 16384 | bytes 65536 | tf_op jit(solution)/shard_map/psum | solution.py:9
  328.3 0.0 copy-start.4
  328.4 0.0 all-gather.10.cloned.1.call-done
  328.4 0.0 copy-done.6
  328.4 2.7 fusion.4
  331.1 0.0 all-gather.12.cloned.1.call-update
  331.1 0.0 all-gather.14.cloned.1.call-start
  331.2 80.5 %all-gather.12.cloned.1.call-done = bf16[1024,1024]{0,1:T(8,128)(2,1)} async-done(((bf16[1024,16]{0,1:T(8,128)(2,1)}), bf16[1024,1024]{0,1:T(8,128)(2,1)}) %all-gather.12.cloned.1.call-update) | async-done | bytes 2097168 | tf_op jit(solution)/shard_map/all_gather | solution.py:49
  411.7 2.6 convolution_convert_fusion
  414.3 0.0 all-gather.14.cloned.1.call-update
  414.3 0.0 all-reduce.3.cloned.1.call-start
  414.4 0.0 slice-start
  414.4 0.0 copy-done.4
  414.4 0.0 copy-start.8
  414.4 2.4 fusion.2
  416.9 0.3 fusion.5
  417.2 26.8 %all_gather.31 = bf16[1024,128]{1,0:T(8,128)(2,1)S(1)} all-gather(bf16[128,128]{1,0:T(8,128)(2,1)S(1)} %fusion.5), channel_id=1, replica_groups=mesh['row'=8,'col'=16,'vox'=4] {'row'}, dimensions={0}, use_global_device_ids=true | all-gather | bytes 294912 | tf_op jit(solution)/shard_map/all_gather | solution.py:71
  444.0 0.7 fusion.3
  444.7 0.8 pad_maximum_fusion
  445.5 0.0 copy-done
  445.6 0.8 dynamic-slice_select_fusion.1
  446.3 0.7 convolution_subtract_fusion.1
  447.1 48.9 %all-gather.14.cloned.1.call-done = bf16[1024,1024]{0,1:T(8,128)(2,1)} async-done(((bf16[1024,16]{0,1:T(8,128)(2,1)}), bf16[1024,1024]{0,1:T(8,128)(2,1)}) %all-gather.14.cloned.1.call-update) | async-done | bytes 2097168 | tf_op jit(solution)/shard_map/all_gather | solution.py:50
  496.0 1.7 dynamic-slice_select_fusion
  497.7 0.0 all-reduce.3.cloned.1.call-update
  497.7 0.8 dynamic-slice_bitcast_fusion.3
  498.4 0.6 pad_maximum_fusion.1
  499.1 3.2 convolution_subtract_fusion
  502.3 75.4 %all-reduce.3.cloned.1.call-done = (bf16[128,1024]{0,1:T(8,128)(2,1)}, bf16[128,1024]{0,1:T(8,128)(2,1)}) async-done(((bf16[128,1024]{0,1:T(8,128)(2,1)}, bf16[128,1024]{0,1:T(8,128)(2,1)}), (bf16[128,1024]{0,1:T(8,128)(2,1)}, bf16[128,1024]{0,1:T(8,128)(2,1)})) %all-reduce.3.cloned.1.call-update) | async-done | bytes 524304 | tf_op jit(solution)/shard_map/psum | solution.py:9
  577.6 1.8 convolution_subtract_fusion.3
  579.5 1.5 convolution_subtract_fusion.2
  (12 shorter events, 0.0 us)
Async XLA Ops:
  7.2 152.4 %copy-start.7 = (bf16[128,16]{0,1:T(8,128)(2,1)S(1)}, bf16[128,16]{0,1:T(8,128)(2,1)}, u32[]{:S(2)}) copy-start(bf16[128,16]{0,1:T(8,128)(2,1)} %param.7) | copy-start | bytes 12292
  7.2 90.2 %all-gather.8.cloned.1.call-start = ((), (), s32[]{:S(2)}) async-start(), calls=%async_computation.1 | async-start | bytes 2129920 | tf_op jit(solution)/shard_map/all_gather | solution.py:30
  7.9 149.0 %all-gather.6.cloned.1.call-start = ((), (), s32[]{:S(2)}) async-start(), calls=%async_computation | async-start | bytes 4718592 | tf_op jit(solution)/shard_map/all_gather | solution.py:26
  8.7 319.7 %copy-start.6 = (bf16[1024,16]{0,1:T(8,128)(2,1)S(1)}, bf16[1024,16]{0,1:T(8,128)(2,1)}, u32[]{:S(2)}) copy-start(bf16[1024,16]{0,1:T(8,128)(2,1)} %param.9) | copy-start | bytes 98308
  8.7 319.7 %all-gather.10.cloned.1.call-start = ((), (), s32[]{:S(2)}) async-start(), calls=%async_computation.2 | async-start | bytes 2129920 | tf_op jit(solution)/shard_map/all_gather | solution.py:33
  159.5 252.2 %all-gather.12.cloned.1.call-start = ((), (), s32[]{:S(2)}) async-start(), calls=%async_computation.3 | async-start | bytes 2129920 | tf_op jit(solution)/shard_map/all_gather | solution.py:49
  328.3 86.1 %copy-start.4 = (bf16[2,1024,128]{2,1,0:T(8,128)(2,1)S(1)}, bf16[2,1024,128]{2,1,0:T(8,128)(2,1)}, u32[]{:S(2)}) copy-start(bf16[2,1024,128]{2,1,0:T(8,128)(2,1)} %param.12) | copy-start | bytes 1572868
  331.1 164.9 %all-gather.14.cloned.1.call-start = ((), (), s32[]{:S(2)}) async-start(), calls=%async_computation.4 | async-start | bytes 2129920 | tf_op jit(solution)/shard_map/all_gather | solution.py:50
  414.3 163.3 %all-reduce.3.cloned.1.call-start = ((), (), s32[]{:S(2)}) async-start(), calls=%async_computation.5 | async-start | bytes 1048576 | tf_op jit(solution)/shard_map/psum | solution.py:9
  414.4 2.5 slice-start
  414.4 29.5 %copy-start.8 = (bf16[2,1024,1024]{2,1,0:T(8,128)(2,1)S(1)}, bf16[2,1024,1024]{2,1,0:T(8,128)(2,1)}, u32[]{:S(2)}) copy-start(bf16[2,1024,1024]{2,1,0:T(8,128)(2,1)} %all-gather.6.cloned.1.call-done) | copy-start | bytes 12582916
  444.0 1.6 copy-start
  444.0 2.4 copy-start.2
  499.1 78.6 %copy-start.3 = (bf16[1024,128]{1,0:T(8,128)(2,1)S(1)}, bf16[1024,128]{1,0:T(8,128)(2,1)}, u32[]{:S(2)}) copy-start(bf16[1024,128]{1,0:T(8,128)(2,1)} %param.10) | copy-start | bytes 786436
  577.6 1.8 copy-start.1
  577.6 1.9 copy-start.5
Sparse Core Ops, SparseCore 0:
  11.4 85.9 all-gather.7
  99.5 57.3 all-gather.5
  160.8 79.4 all-gather.9
  331.2 80.4 all-gather.11
  415.5 80.4 all-gather.13
  498.8 78.8 all-reduce.2
where the time goes:
time: 588 us
  waiting for transfers between devices  354 us (60%)
  blocking collectives  194 us (33%)
  matrix products  19.5 us (3%)
  between operations  14.3 us (2%)
    all_gather x1, waiting for transfers between devices, per_device(): lax.all_gather(panel_low, ('col', 'vox'), axis=1, tiled=True)  88.6 us
    all_gather x1, waiting for transfers between devices, per_device(): lax.all_gather(updated, ('col', 'vox'), axis=1, tiled=True)  80.5 us
    psum x1, waiting for transfers between devices, spread(): return lax.psum(block, axis)  75.4 us
    all_gather x1, blocking collectives, per_device(): lax.all_gather(panel_top, ('col', 'vox'), axis=1, tiled=True)  69.7 us
    all_gather x1, blocking collectives, per_device(): lax.all_gather(own_top.astype(jnp.bfloat16), ('col', 'vox'), axis=1, tile...  66.4 us
    all_gather x1, waiting for transfers between devices, per_device(): whole_inverses = lax.all_gather(inverses, 'row', axis=1, tiled=True)  59.5 us
    all_gather x1, waiting for transfers between devices, per_device(): lax.all_gather(own_next.astype(jnp.bfloat16), ('col', 'vox'), axis=1, til...  48.9 us
    psum x1, blocking collectives, spread(): return lax.psum(block, axis)  31.6 us
  transfers between devices with their start and end apart: 6, of which 5 were waited for; matrix products, arithmetic and copies ran while one was open for 2% of the time, Pallas kernels for 0%

commit v1 on v0

--- a/solution.py
+++ b/solution.py
@@ -23,7 +23,10 @@
     low_rows = panel_low.shape[0]
     rest_cols = gram_rest.shape[1]
     root_row = col_index * rest_cols // low_rows
-    whole_inverses = lax.all_gather(inverses, "row", axis=1, tiled=True)
+    devices = lax.axis_size("row")
+    pieces = jnp.stack([inverses for _ in range(devices)])
+    pieces = lax.all_to_all(pieces, "row", split_axis=0, concat_axis=0)
+    whole_inverses = jnp.concatenate(pieces, axis=1)
     own_rows = lax.dynamic_slice_in_dim(whole_inverses, col_index * col_width, col_width, 1)
     rows_used = own_rows[0]
     own_top = contract(lax.all_gather(panel_top, ("col", "vox"), axis=1, tiled=True), rows_used)

time: 588 us -> 552 us (0.939)
  waiting for transfers between devices: 354 us -> 298 us
  local copies, waits for them, and re-layouts: 0.85 us -> 12 us
  starting transfers between devices: 0.24 us -> 10.5 us
    all_to_all x0 -> x1, waiting for transfers between devices: none -> 95.5 us  [per_device(): pieces = lax.all_to_all(pieces, 'row', split_axis=0, concat_axis=0)]
    all_gather x1, waiting for transfers between devices: 88.6 us -> 0.01 us  [per_device(): lax.all_gather(panel_low, ('col', 'vox'), axis=1, tiled=True)]
    all_gather x1 -> x0, waiting for transfers between devices: 59.5 us -> none  [per_device(): whole_inverses = lax.all_gather(inverses, 'row', axis=1, tiled=True)]
    all_to_all x0 -> x1, starting transfers between devices: none -> 10.3 us  [per_device(): pieces = lax.all_to_all(pieces, 'row', split_axis=0, concat_axis=0)]
  transfers between devices with their start and end apart: 6 -> 6, of which waited for: 5 -> 4; matrix products, arithmetic and copies ran while one was open for 2% -> 3% of each run, Pallas kernels for 0% -> 0%
where the time goes in v1:
time: 552 us; the launch traced here: 551 us
  waiting for transfers between devices  298 us (54%)
  blocking collectives  195 us (35%)
  matrix products  17.7 us (3%)
  between operations  14 us (3%)
  local copies, waits for them, and re-layouts  12 us (2%)
  starting transfers between devices  10.5 us (2%)
    all_to_all x1, waiting for transfers between devices, per_device(): pieces = lax.all_to_all(pieces, 'row', split_axis=0, concat_axis=0)  95.5 us
    all_gather x1, waiting for transfers between devices, per_device(): lax.all_gather(updated, ('col', 'vox'), axis=1, tiled=True)  78.8 us
    psum x1, waiting for transfers between devices, spread(): return lax.psum(block, axis)  75.4 us
    all_gather x1, blocking collectives, per_device(): lax.all_gather(panel_top, ('col', 'vox'), axis=1, tiled=True)  68.8 us
    all_gather x1, blocking collectives, per_device(): lax.all_gather(own_top.astype(jnp.bfloat16), ('col', 'vox'), axis=1, tile...  67 us
    all_gather x1, waiting for transfers between devices, per_device(): lax.all_gather(own_next.astype(jnp.bfloat16), ('col', 'vox'), axis=1, til...  47.6 us
    psum x1, blocking collectives, spread(): return lax.psum(block, axis)  31.9 us
    all_gather x1, blocking collectives, per_device(): top_new = lax.all_gather(top_part, 'row', axis=0, tiled=True)  26.9 us
  transfers between devices with their start and end apart: 6, of which 4 were waited for; matrix products, arithmetic and copies ran while one was open for 3% of the time, Pallas kernels for 0%

profile of v1, /device:TPU:2, one launch (start us, length us, event | category | flops | bytes accessed | tf_op | source)
XLA Modules:
  0.0 550.9 jit_solution(15810987058612879693)
XLA Ops:
  7.2 3.5 stack.14
  10.7 10.3 %all-to-all-start = ((bf16[8,2,128,1024]{3,2,1,0:T(8,128)(2,1)}), bf16[8,2,128,1024]{3,2,1,0:T(8,128)(2,1)}, u32[]{:S(2)}, u32[]{:S(2)}) async-start(bf16[8,2,128,1024]{3,2,1,0:T(8,128)(2,1)} %stack.14), calls=%async_computation | async-start | bytes 8388608 | tf_op jit(solution)/shard_map/all_to_all | solution.py:28
  21.0 0.0 all-gather.5.cloned.1.call-start
  21.1 0.7 all-gather.5.cloned.1.call-update
  21.7 0.0 all-gather.7.cloned.1.call-start
  21.8 95.5 %all-to-all-done = bf16[8,2,128,1024]{3,2,1,0:T(8,128)(2,1)} async-done(((bf16[8,2,128,1024]{3,2,1,0:T(8,128)(2,1)}), bf16[8,2,128,1024]{3,2,1,0:T(8,128)(2,1)}, u32[]{:S(2)}, u32[]{:S(2)}) %all-to-all-start) | async-done | bytes 4194336 | tf_op jit(solution)/shard_map/all_to_all | solution.py:28
  117.3 4.7 copy.18
  122.0 2.6 fusion.2
  124.6 0.0 all-gather.7.cloned.1.call-update
  124.7 0.0 all-gather.9.cloned.1.call-start
  124.7 0.0 copy-done.7
  124.8 68.8 %all_gather.23 = bf16[128,1024]{0,1:T(8,128)(2,1)S(1)} all-gather(bf16[128,16]{0,1:T(8,128)(2,1)S(1)} %copy-done.7), channel_id=1, replica_groups=mesh['row'=8,'col'=16,'vox'=4] {'col','vox'}, dimensions={1}, use_global_device_ids=true | all-gather | bytes 266240 | tf_op jit(solution)/shard_map/all_gather | solution.py:32
  193.6 0.9 fusion.3
  194.5 67.0 %all_gather.24 = bf16[128,1024]{0,1:T(8,128)(2,1)S(1)} all-gather(bf16[128,16]{0,1:T(8,128)(2,1)S(1)} %fusion.3), channel_id=1, replica_groups=mesh['row'=8,'col'=16,'vox'=4] {'col','vox'}, dimensions={1}, use_global_device_ids=true | all-gather | bytes 266240 | tf_op jit(solution)/shard_map/all_gather | solution.py:35
  261.4 0.1 dynamic-slice_select_fusion.2
  261.6 31.9 %psum.21 = bf16[16,1024]{0,1:T(8,128)(2,1)S(1)} all-reduce(bf16[16,1024]{0,1:T(8,128)(2,1)S(1)} %dynamic-slice_select_fusion.2), channel_id=1, replica_groups=mesh['row'=8,'col'=16,'vox'=4] {'row'}, use_global_device_ids=true, to_apply=%region_0.1 | all-reduce | flops 16384 | bytes 65536 | tf_op jit(solution)/shard_map/psum | solution.py:9
  293.5 0.0 all-gather.7.cloned.1.call-done
  293.5 0.0 copy-done.6
  293.5 2.6 fusion
  296.2 0.0 all-gather.9.cloned.1.call-update
  296.2 0.0 all-gather.11.cloned.1.call-start
  296.2 78.8 %all-gather.9.cloned.1.call-done = bf16[1024,1024]{0,1:T(8,128)(2,1)} async-done(((bf16[1024,16]{0,1:T(8,128)(2,1)}), bf16[1024,1024]{0,1:T(8,128)(2,1)}) %all-gather.9.cloned.1.call-update) | async-done | bytes 2097168 | tf_op jit(solution)/shard_map/all_gather | solution.py:52
  375.0 2.6 convolution_convert_fusion.2
  377.6 0.0 all-gather.11.cloned.1.call-update
  377.6 0.0 all-reduce.3.cloned.1.call-start
  377.7 0.0 copy-start.4
  377.7 2.8 fusion.9
  380.5 0.0 slice-start
  380.5 0.0 copy-done.4
  380.5 0.7 convolution_convert_fusion.1
  381.2 0.2 slice-done
  381.4 0.3 fusion.1
  381.7 0.0 copy-start
  381.7 26.9 %all_gather.27 = bf16[1024,128]{1,0:T(8,128)(2,1)S(1)} all-gather(bf16[128,128]{1,0:T(8,128)(2,1)S(1)} %fusion.1), channel_id=1, replica_groups=mesh['row'=8,'col'=16,'vox'=4] {'row'}, dimensions={0}, use_global_device_ids=true | all-gather | bytes 294912 | tf_op jit(solution)/shard_map/all_gather | solution.py:74
  408.6 0.7 convolution_convert_fusion
  409.4 0.8 pad_maximum_fusion
  410.2 0.0 copy-done
  410.2 0.8 dynamic-slice_select_fusion.1
  411.0 0.7 convolution_subtract_fusion.1
  411.7 47.6 %all-gather.11.cloned.1.call-done = bf16[1024,1024]{0,1:T(8,128)(2,1)} async-done(((bf16[1024,16]{0,1:T(8,128)(2,1)}), bf16[1024,1024]{0,1:T(8,128)(2,1)}) %all-gather.11.cloned.1.call-update) | async-done | bytes 2097168 | tf_op jit(solution)/shard_map/all_gather | solution.py:53
  459.3 1.7 dynamic-slice_select_fusion
  461.0 0.0 all-reduce.3.cloned.1.call-update
  461.0 0.8 dynamic-slice_bitcast_fusion.3
  461.8 0.6 pad_maximum_fusion.1
  462.4 3.2 convolution_subtract_fusion
  465.6 75.4 %all-reduce.3.cloned.1.call-done = (bf16[128,1024]{0,1:T(8,128)(2,1)}, bf16[128,1024]{0,1:T(8,128)(2,1)}) async-done(((bf16[128,1024]{0,1:T(8,128)(2,1)}, bf16[128,1024]{0,1:T(8,128)(2,1)}), (bf16[128,1024]{0,1:T(8,128)(2,1)}, bf16[128,1024]{0,1:T(8,128)(2,1)})) %all-reduce.3.cloned.1.call-update) | async-done | bytes 524304 | tf_op jit(solution)/shard_map/psum | solution.py:9
  541.0 1.8 convolution_subtract_fusion.3
  542.8 1.5 convolution_subtract_fusion.2
  (12 shorter events, 0.0 us)
Async XLA Ops:
  10.7 106.6 %all-to-all-start = ((bf16[8,2,128,1024]{3,2,1,0:T(8,128)(2,1)}), bf16[8,2,128,1024]{3,2,1,0:T(8,128)(2,1)}, u32[]{:S(2)}, u32[]{:S(2)}) async-start(bf16[8,2,128,1024]{3,2,1,0:T(8,128)(2,1)} %stack.14), calls=%async_computation | async-start | bytes 8388608 | tf_op jit(solution)/shard_map/all_to_all | solution.py:28
  21.0 101.0 %all-gather.5.cloned.1.call-start = ((), (), s32[]{:S(2)}) async-start(), calls=%async_computation.1 | async-start | bytes 2129920 | tf_op jit(solution)/shard_map/all_gather | solution.py:33
  21.7 271.8 %all-gather.7.cloned.1.call-start = ((), (), s32[]{:S(2)}) async-start(), calls=%async_computation.2 | async-start | bytes 2129920 | tf_op jit(solution)/shard_map/all_gather | solution.py:36
  122.0 2.8 copy-start.7
  122.0 171.5 %copy-start.6 = (bf16[1024,16]{0,1:T(8,128)(2,1)S(1)}, bf16[1024,16]{0,1:T(8,128)(2,1)}, u32[]{:S(2)}) copy-start(bf16[1024,16]{0,1:T(8,128)(2,1)} %param.9) | copy-start | bytes 98308
  124.7 250.3 %all-gather.9.cloned.1.call-start = ((), (), s32[]{:S(2)}) async-start(), calls=%async_computation.3 | async-start | bytes 2129920 | tf_op jit(solution)/shard_map/all_gather | solution.py:52
  296.2 163.1 %all-gather.11.cloned.1.call-start = ((), (), s32[]{:S(2)}) async-start(), calls=%async_computation.4 | async-start | bytes 2129920 | tf_op jit(solution)/shard_map/all_gather | solution.py:53
  377.6 163.3 %all-reduce.3.cloned.1.call-start = ((), (), s32[]{:S(2)}) async-start(), calls=%async_computation.5 | async-start | bytes 1048576 | tf_op jit(solution)/shard_map/psum | solution.py:9
  377.7 2.8 copy-start.4
  380.5 1.0 slice-start
  381.7 28.5 %copy-start = (bf16[1024,1024]{0,1:T(8,128)(2,1)S(1)}, bf16[1024,1024]{0,1:T(8,128)(2,1)}, u32[]{:S(2)}) copy-start(bf16[1024,1024]{0,1:T(8,128)(2,1)} %all-gather.7.cloned.1.call-done) | copy-start | bytes 6291460
  408.6 2.3 copy-start.2
  462.4 78.5 %copy-start.3 = (bf16[1024,128]{1,0:T(8,128)(2,1)S(1)}, bf16[1024,128]{1,0:T(8,128)(2,1)}, u32[]{:S(2)}) copy-start(bf16[1024,128]{1,0:T(8,128)(2,1)} %param.10) | copy-start | bytes 786436
  540.9 1.8 copy-start.1
  540.9 1.9 copy-start.5
Sparse Core Ops, SparseCore 0:
  25.2 82.7 all-gather.4
  124.8 77.6 all-gather.6
  296.3 78.6 all-gather.8
  378.8 80.4 all-gather.10
  462.1 78.8 all-reduce.2
